TPU v7x, 512 devices: a whole 4x8x8 slice. The times are simulated.
512 devices in a mesh: rep: 4 (over x), exp: 128 (over z, y, core).
Axes of the slice: x: 4, y: 8, z: 8, core: 2. Of those that a mesh axis runs over, the one named last changes fastest.
Arguments:
- tokens: bfloat16 [16384, 2048], P('exp', 'rep'), may hold values from -6 to 6
- expert_ids: int32 [16384, 8], P('exp'), may hold values from 0 to 127, all different within a row; in each aligned block of 128 rows (0 to 127, 128 to 255, ...) at most 12 rows name the same one
- route_weights: float32 [16384, 8], P('exp'), may hold values from 0.05 to 1
- w_gate: bfloat16 [128, 768, 2048], P('exp', None, 'rep'), may hold values from -0.125 to 0.125
- w_up: bfloat16 [128, 768, 2048], P('exp', None, 'rep'), may hold values from -0.125 to 0.125
- w_down: bfloat16 [128, 768, 2048], P('exp', None, 'rep'), may hold values from -0.21875 to 0.21875
Outputs:
- mixed: bfloat16 [16384, 2048], P('exp', 'rep')
Inputs may be any that keep to these rules, and one draw needn't show every extreme that they name: `expert_ids`: each token names 8 different experts. Within the rows of one index of exp (aligned blocks of 128 tokens) no expert is named more than 12 times, a bound that some block reaches.
All inputs are finite; a program needn't handle non-finite values.
Results may differ from a plain program's by a relative error of at most 0.0058.
Values may be sent and summed in bfloat16 or wider, within the bound.
A program may use at most 64 MiB of HBM per device.

v0:
```python
import jax
import jax.numpy as jnp
from jax import lax
from jax.sharding import PartitionSpec as P

EXPERTS = 128


def local(tokens, expert_ids, route_weights, w_gate, w_up, w_down):
    tok_rows = expert_ids.shape[0]
    top_count = expert_ids.shape[1]
    local_experts = w_gate.shape[0]
    replicas = lax.axis_size("rep")
    replica_index = lax.axis_index("rep")
    full_cap = replicas * max(1, tok_rows * top_count * 3 // (8 * EXPERTS))
    slot_cap = full_cap // replicas
    assigned = expert_ids.reshape(-1)
    onehot = (assigned[:, None] == jnp.arange(EXPERTS, dtype=jnp.int32)[None, :]).astype(jnp.int32)
    before = jnp.cumsum(onehot, axis=0) - onehot
    slot_ids = jnp.sum(before * onehot, axis=1)
    owned = slot_ids % replicas == replica_index
    target = assigned * slot_cap + slot_ids // replicas
    destination = jnp.where(owned, target, EXPERTS * slot_cap)
    probs = route_weights / jnp.sum(route_weights, axis=1, keepdims=True)
    full_rows = lax.all_gather(tokens, "rep", axis=1, tiled=True)
    width = full_rows.shape[1]
    repeated = jnp.repeat(full_rows, top_count, axis=0)
    outgoing = (
        jnp.zeros((EXPERTS * slot_cap, width), jnp.bfloat16)
        .at[destination]
        .set(repeated, mode="drop")
    )
    outgoing = outgoing.reshape(EXPERTS, slot_cap, width)
    arrived = lax.all_to_all(outgoing, "exp", split_axis=0, concat_axis=1, tiled=True)
    gate_sum = jnp.einsum(
        "esd,efd->esf",
        arrived,
        lax.all_gather(w_gate, "rep", axis=2, tiled=True),
        preferred_element_type=jnp.float32,
    )
    up_sum = jnp.einsum(
        "esd,efd->esf",
        arrived,
        lax.all_gather(w_up, "rep", axis=2, tiled=True),
        preferred_element_type=jnp.float32,
    )
    hidden = (jax.nn.silu(gate_sum) * up_sum).astype(jnp.bfloat16)
    expert_out = jnp.einsum(
        "esf,efd->esd",
        hidden,
        lax.all_gather(w_down, "rep", axis=2, tiled=True),
        preferred_element_type=jnp.float32,
    ).astype(jnp.bfloat16)
    owners = expert_out.shape[1] // slot_cap
    share = width // replicas
    split_out = expert_out.reshape(local_experts, owners, slot_cap, replicas, share)
    homed = lax.all_to_all(
        lax.all_to_all(split_out, "rep", split_axis=3, concat_axis=3, tiled=True),
        "exp",
        split_axis=1,
        concat_axis=1,
        tiled=True,
    )
    ordered = jnp.swapaxes(homed, 0, 1).reshape(EXPERTS * full_cap, share)
    picked = ordered[assigned * full_cap + slot_ids].astype(jnp.float32)
    weighted = picked.reshape(tok_rows, top_count, share) * probs[:, :, None]
    return jnp.sum(weighted, axis=1).astype(jnp.bfloat16)


def solution(mesh):
    return jax.shard_map(
        local,
        mesh=mesh,
        in_specs=(
            P("exp", "rep"),
            P("exp", None),
            P("exp", None),
            P("exp", None, "rep"),
            P("exp", None, "rep"),
            P("exp", None, "rep"),
        ),
        out_specs=P("exp", "rep"),
        check_vma=False,
    )
```

profile of v0, /device:TPU:1, one launch (start us, length us, event | category | flops | bytes accessed | tf_op | source)
XLA Modules:
  0.0 255.8 jit_solution(238828360793560490)
XLA Ops:
  6.5 0.7 all-gather.4.cloned.1.call-update
  7.3 0.7 all-gather.6.cloned.1.call-update
  8.1 0.7 all-gather.8.cloned.1.call-update
  8.8 0.1 copy.24
  8.9 0.1 eq.44
  8.9 0.1 eq.40
  9.0 0.1 copy.26
  9.1 0.2 fusion.25
  9.5 0.1 copy.27
  9.6 0.1 copy.28
  9.7 0.1 mul.52
  9.8 0.1 copy.31
  9.9 0.1 mul.57
  10.0 0.4 fusion.24
  10.4 11.1 %all_gather.12 = bf16[128,2048]{1,0:T(8,128)(2,1)S(1)} all-gather(bf16[128,512]{1,0:T(8,128)(2,1)S(1)} %copy-done), channel_id=1, replica_groups=mesh['rep'=4,'exp'=128] {'rep'}, dimensions={1}, use_global_device_ids=true | all-gather | bytes 655360 | tf_op jit(solution)/shard_map/all_gather | solution.py:25
  21.5 7.7 %scatter_custom_fusion = bf16[384,2048]{1,0:T(8,128)(2,1)} fusion(s32[1024]{0:T(1024)S(1)} %bitcast.42, bf16[128,2048]{1,0:T(8,128)(2,1)S(1)} %all_gather.12, bf16[]{:T(256)} %constant.41.clone.1), kind=kCustom, calls=%fused_computation.2 | custom fusion | bytes 2097154 | tf_op jit(solution)/shard_map/scatter | solution.py:31
  29.1 4.1 %reshape.193 = bf16[128,3,2048]{2,1,0:T(4,128)(2,1)S(1)} reshape(bf16[384,2048]{1,0:T(8,128)(2,1)} %scatter_custom_fusion) | data formatting | bytes 3145728 | tf_op jit(solution)/shard_map/reshape | solution.py:33
  33.2 71.6 %all_to_all.19 = bf16[128,3,2048]{2,1,0:T(4,128)(2,1)} all-to-all(bf16[128,3,2048]{2,1,0:T(4,128)(2,1)S(1)} %reshape.193), channel_id=1, replica_groups=mesh['rep'=4,'exp'=128] {'exp'}, dimensions={0} | all-to-all | bytes 3145728 | tf_op jit(solution)/shard_map/all_to_all | solution.py:34
  104.8 3.9 %reshape.194 = bf16[384,2048]{1,0:T(8,128)(2,1)S(1)} reshape(bf16[128,3,2048]{2,1,0:T(4,128)(2,1)} %all_to_all.19) | data formatting | bytes 3145728 | tf_op jit(solution)/shard_map/reshape.10
  108.7 4.4 %fusion.6 = f32[384,768]{1,0:T(8,128)} fusion(bf16[384,2048]{1,0:T(8,128)(2,1)S(1)} %reshape.194, bf16[1,768,2048]{2,1,0:T(8,128)(2,1)} %all-gather.4.cloned.1.call-done), kind=kOutput, calls=%fused_computation.8 | convolution fusion | flops 1207959552 | bytes 5898240 | tf_op jit(solution)/shard_map/esd,efd->esf/dot_general | solution.py:35
  113.2 40.8 %all-gather.8.cloned.1.call-done = bf16[1,768,2048]{2,1,0:T(8,128)(2,1)} async-done(((bf16[1,768,512]{2,1,0:T(8,128)(2,1)}), bf16[1,768,2048]{2,1,0:T(8,128)(2,1)}) %all-gather.8.cloned.1.call-update) | async-done | bytes 3145744 | tf_op jit(solution)/shard_map/all_gather | solution.py:51
  153.9 6.3 %fusion.8 = bf16[384,2048]{1,0:T(8,128)(2,1)S(1)} fusion(bf16[1,768,2048]{2,1,0:T(8,128)(2,1)} %all-gather.8.cloned.1.call-done, bf16[384,2048]{1,0:T(8,128)(2,1)S(1)} %reshape.194, bf16[1,768,2048]{2,1,0:T(8,128)(2,1)} %all-gather.6.cloned.1.call-done, f32[384,768]{1,0:T(8,128)} %fusion.6), kind=kOutput, calls=%fused_computation.10 | convolution fusion | flops 2418475008 | bytes 10616832 | tf_op jit(solution)/shard_map/esf,efd->esd/dot_general | solution.py:48
  160.3 1.2 reshape.198
  161.5 0.3 copy.29
  161.8 22.4 %all_to_all.20 = bf16[1,128,3,4,512]{4,1,2,0,3:T(8,128)(2,1)S(1)} all-to-all(bf16[1,128,3,4,512]{4,1,2,0,3:T(8,128)(2,1)S(1)} %copy.29), channel_id=1, replica_groups=mesh['rep'=4,'exp'=128] {'rep'}, dimensions={3} | all-to-all | bytes 3145728 | tf_op jit(solution)/shard_map/all_to_all | solution.py:58
  184.2 2.4 copy.30
  186.6 15.7 %all-to-all-start.2 = ((bf16[1,128,3,4,512]{4,3,2,0,1:T(4,128)(2,1)}), bf16[1,128,3,4,512]{4,3,2,0,1:T(4,128)(2,1)S(1)}, u32[]{:S(2)}, u32[]{:S(2)}) async-start(bf16[1,128,3,4,512]{4,3,2,0,1:T(4,128)(2,1)} %copy.30), calls=%async_computation.2 | async-start | bytes 3145728 | tf_op jit(solution)/shard_map/all_to_all | solution.py:57
  202.3 0.1 copy.32
  202.4 41.1 %all-to-all-done.2 = bf16[1,128,3,4,512]{4,3,2,0,1:T(4,128)(2,1)S(1)} async-done(((bf16[1,128,3,4,512]{4,3,2,0,1:T(4,128)(2,1)}), bf16[1,128,3,4,512]{4,3,2,0,1:T(4,128)(2,1)S(1)}, u32[]{:S(2)}, u32[]{:S(2)}) %all-to-all-start.2) | async-done | bytes 1572896 | tf_op jit(solution)/shard_map/all_to_all | solution.py:57
  243.5 0.4 reshape_transpose.3
  243.9 4.0 %gather_fusion = bf16[1024,512]{1,0:T(8,128)(2,1)S(1)} fusion(bf16[1536,512]{1,0:T(8,128)(2,1)S(1)} %reshape_transpose.3, s32[1024]{0:T(1024)S(1)} %broadcast_clamp_fusion), kind=kCustom, calls=%fused_computation | custom fusion | bytes 2101248 | tf_op jit(solution)/shard_map/gather | solution.py:65
  247.9 1.3 fusion.11
  (20 shorter events, 0.3 us)
Async XLA Ops:
  6.5 2.2 copy-start.1
  6.5 102.2 %all-gather.4.cloned.1.call-start = ((), (), s32[]{:S(2)}) async-start(), calls=%async_computation.3 | async-start | bytes 3932160 | tf_op jit(solution)/shard_map/all_gather | solution.py:38
  7.3 105.9 %all-gather.6.cloned.1.call-start = ((), (), s32[]{:S(2)}) async-start(), calls=%async_computation.4 | async-start | bytes 3932160 | tf_op jit(solution)/shard_map/all_gather | solution.py:44
  8.0 145.9 %all-gather.8.cloned.1.call-start = ((), (), s32[]{:S(2)}) async-start(), calls=%async_computation.5 | async-start | bytes 3932160 | tf_op jit(solution)/shard_map/all_gather | solution.py:51
  9.4 1.0 copy-start
  186.6 15.7 %copy-start.2 = (f32[128,8]{0,1:T(8,128)S(1)}, f32[128,8]{0,1:T(8,128)}, u32[]{:S(2)}) copy-start(f32[128,8]{0,1:T(8,128)} %param.8) | copy-start | bytes 12292
  186.6 57.0 %all-to-all-start.2 = ((bf16[1,128,3,4,512]{4,3,2,0,1:T(4,128)(2,1)}), bf16[1,128,3,4,512]{4,3,2,0,1:T(4,128)(2,1)S(1)}, u32[]{:S(2)}, u32[]{:S(2)}) async-start(bf16[1,128,3,4,512]{4,3,2,0,1:T(4,128)(2,1)} %copy.30), calls=%async_computation.2 | async-start | bytes 3145728 | tf_op jit(solution)/shard_map/all_to_all | solution.py:57
Sparse Core Ops, SparseCore 0:
  9.4 50.1 all-gather.3
  61.7 45.0 all-gather.5
  108.9 45.0 all-gather.7
where the time goes:
time: 257 us; the launch traced here: 256 us
  blocking collectives  105 us (41%)
  waiting for transfers between devices  84 us (33%)
  local copies, waits for them, and re-layouts  24.9 us (10%)
  starting transfers between devices  15.8 us (6%)
  between operations  13.3 us (5%)
  matrix products  10.7 us (4%)
    all_to_all x1, blocking collectives, local(): lax.all_to_all(outgoing, 'exp', split_axis=0, concat_axis=1, tiled=True)  71.6 us
    all_to_all x1, waiting for transfers between devices, local(): lax.all_to_all(lax.all_to_all(split_out, 'rep', split_axis=3, concat_axis...  41.1 us
    all_gather x1, waiting for transfers between devices, local(): lax.all_gather(w_down, 'rep', axis=2, tiled=True)  40.8 us
    all_to_all x1, blocking collectives, local(): lax.all_to_all(split_out, 'rep', split_axis=3, concat_axis=3, tiled=True)  22.4 us
    all_to_all x1, starting transfers between devices, local(): lax.all_to_all(lax.all_to_all(split_out, 'rep', split_axis=3, concat_axis...  15.7 us
    all_gather x1, blocking collectives, local(): full_rows = lax.all_gather(tokens, 'rep', axis=1, tiled=True)  11.1 us
    scatter x1, local copies, waits for them, and re-layouts, local(): outgoing = jnp.zeros((EXPERTS * slot_cap, width), jnp.bfloat16).at[destin...  7.66 us
    dot_general x1, matrix products, local(): jnp.einsum('esf,efd->esd', hidden, lax.all_gather(w_down, 'rep', axis=2,...  6.33 us
  transfers between devices with their start and end apart: 4, of which 2 were waited for; matrix products, arithmetic and copies ran while one was open for 8% of the time, Pallas kernels for 0%

commit v1 on v0

v1 whole, which is shorter than its diff:
```python
import functools

import jax
import jax.numpy as jnp
from jax import lax
from jax.experimental import pallas as pl
from jax.experimental.pallas import tpu as pltpu
from jax.sharding import PartitionSpec as P

MESH = pl.DeviceIdType.MESH
BF16 = jnp.bfloat16
F32 = jnp.float32
CAP = 12
QUADS = 3
SPAN = 16
LANES = 128
BLOCKS = 4
CORES = 2
STAGES = 5


def signed_step(place, size):
    return (size + (1 - 2 * ((place + 1) % 2)) * ((place + 1) // 2)) % size


def place_of(offset, size):
    return jnp.where(
        offset == 0, 0, jnp.where(2 * offset <= size, 2 * offset - 1, 2 * (size - offset))
    )


def dot(a, b):
    return jnp.dot(a, b, preferred_element_type=F32)


def dot_t(a, b):
    return lax.dot_general(a, b, (((1,), (1,)), ((), ())), preferred_element_type=F32)


def kernel(
    sizes,
    tok,
    ids,
    route,
    wg_any,
    wu_any,
    wd_any,
    out,
    wg,
    wu,
    wd,
    perm,
    perm_t,
    slot_t,
    slot_tok,
    prob_tok,
    send,
    recv,
    back,
    home,
    table,
    part,
    part16,
    far_in,
    near_in,
    relay,
    relay_in,
    hid,
    w_sem,
    send_sem,
    recv_sem,
    back_sem,
    home_sem,
    x_send,
    x_recv,
):
    n_z, n_y, n_rep = sizes
    experts = n_z * SPAN
    ff = wg.shape[0]
    half = ff // 2
    quarter = SPAN * CAP // n_rep
    me, rep = lax.axis_index("exp"), lax.axis_index("rep")
    my_z, my_y, my_c = me // SPAN, (me // CORES) % n_y, me % CORES
    right, left, opp = (rep + 1) % n_rep, (rep + n_rep - 1) % n_rep, (rep + 2) % n_rep

    def peer(k, sign):
        place_z, place_y, flip = k // SPAN, (k % SPAN) // CORES, k % CORES
        z = (my_z + n_z + sign * signed_step(place_z, n_z)) % n_z
        y = (my_y + n_y + sign * signed_step(place_y, n_y)) % n_y
        return (z * n_y + y) * CORES + (my_c + flip) % CORES

    barrier = pltpu.get_barrier_semaphore()

    @pl.loop(1, experts)
    def _(k):
        pl.semaphore_signal(barrier, inc=1, device_id={"exp": peer(k, 1)}, device_id_type=MESH)

    for side in (left, right):
        pl.semaphore_signal(barrier, inc=1, device_id={"rep": side}, device_id_type=MESH)

    weights = [
        pltpu.make_async_copy(src.at[0], dst, w_sem.at[i])
        for i, (src, dst) in enumerate(((wg_any, wg), (wu_any, wu), (wd_any, wd)))
    ]
    for copy in weights:
        copy.start()

    row = lax.broadcasted_iota(jnp.int32, (256, 256), 0)
    col = lax.broadcasted_iota(jnp.int32, (256, 256), 1)
    perm[...] = (
        col == (row & 3) * 64 + ((row >> 2) & 3) * 16 + (row >> 4)
    ).astype(F32).astype(BF16)
    perm_t[...] = (
        row == (col & 3) * 64 + ((col >> 2) & 3) * 16 + (col >> 4)
    ).astype(F32).astype(BF16)

    chosen = ids[...]
    rows = chosen.shape[0]
    off_z = ((chosen >> 4) - my_z + n_z) & (n_z - 1)
    off_y = (((chosen >> 1) & (n_y - 1)) - my_y + n_y) & (n_y - 1)
    off_c = ((chosen & 1) - my_c + CORES) & 1
    number = place_of(off_z, n_z) * SPAN + place_of(off_y, n_y) * CORES + off_c
    probs = route[...] / jnp.sum(route[...], axis=1, keepdims=True)
    lane = lax.broadcasted_iota(jnp.int32, (rows, experts), 1)
    named = jnp.zeros((rows, experts), F32)
    prob = jnp.zeros((rows, experts), F32)
    for j in range(chosen.shape[1]):
        hit = number[:, j : j + 1] == lane
        named = named + jnp.where(hit, 1.0, 0.0)
        prob = prob + jnp.where(hit, probs[:, j : j + 1], 0.0)
    t_row = lax.broadcasted_iota(jnp.int32, (rows, rows), 0)
    t_col = lax.broadcasted_iota(jnp.int32, (rows, rows), 1)
    below = (t_col < t_row).astype(F32).astype(BF16)
    slot = dot(below, named.astype(BF16))
    slot = jnp.where(named > 0.5, slot, -1.0)
    slot_tok[...] = slot
    prob_tok[...] = prob
    slot_t[...] = slot.T

    pl.semaphore_wait(barrier, experts + 1)

    def pack(rows2d, place, g):
        stacked = jnp.concatenate(
            [
                jnp.concatenate(
                    [rows2d[64 * q : 64 * q + 64, LANES * b : LANES * (b + 1)] for b in range(BLOCKS)],
                    axis=0,
                )
                for q in range(QUADS)
            ],
            axis=1,
        )
        tiles = dot(perm[...], stacked).astype(BF16)
        for q in range(QUADS):
            place[pl.ds(g * SPAN, SPAN), q] = tiles[:, LANES * q : LANES * (q + 1)].reshape(
                SPAN, SPAN, LANES
            )

    def unpack(place, g):
        tiles = jnp.concatenate(
            [place[pl.ds(g * SPAN, SPAN), q].reshape(256, LANES) for q in range(QUADS)], axis=1
        )
        return dot(perm_t[...], tiles).astype(BF16)

    @pl.loop(0, n_z)
    def _(g):
        slots = slot_t[pl.ds(g * SPAN, SPAN), :]
        onehot = jnp.concatenate(
            [(slots == float(s)).astype(F32).astype(BF16) for s in range(CAP)], axis=0
        )
        pack(dot(onehot, tok[...]).astype(BF16), send, g)

        @pl.loop(0, SPAN)
        def _(h):
            k = g * SPAN + h

            @pl.when(k > 0)
            def _():
                pltpu.make_async_remote_copy(
                    src_ref=send.at[k],
                    dst_ref=recv.at[k],
                    send_sem=send_sem,
                    recv_sem=recv_sem.at[g],
                    device_id={"exp": peer(k, 1)},
                    device_id_type=MESH,
                ).start()

            @pl.when(k == 0)
            def _():
                pltpu.make_async_copy(send.at[0], recv.at[0], recv_sem.at[0]).start()

    for copy in weights:
        copy.wait()

    def across(kind, c, src, dst, side):
        return pltpu.make_async_remote_copy(
            src_ref=src,
            dst_ref=dst,
            send_sem=x_send.at[kind, c],
            recv_sem=x_recv.at[kind, c],
            device_id={"rep": side},
            device_id_type=MESH,
        )

    def far(c):
        return (
            across(0, c, part16.at[0, c, opp], far_in.at[0, c], right),
            across(1, c, part16.at[1, c, opp], far_in.at[1, c], left),
        )

    def near(c):
        return (
            across(2, c, part16.at[1, c, right], near_in.at[1, c], right),
            across(3, c, part16.at[0, c, left], near_in.at[0, c], left),
        )

    def relayed(c):
        return (
            across(4, c, relay.at[0, c], relay_in.at[0, c], right),
            across(5, c, relay.at[1, c], relay_in.at[1, c], left),
        )

    def hidden_out(c):
        return (
            across(6, c, hid.at[c, rep], hid.at[c, rep], right),
            across(7, c, hid.at[c, rep], hid.at[c, rep], left),
        )

    def hidden_in(c):
        return (
            across(6, c, hid.at[c, left], hid.at[c, left], right),
            across(7, c, hid.at[c, right], hid.at[c, right], left),
        )

    def onward(c):
        return (
            across(8, c, hid.at[c, left, :, pl.ds(0, half)], hid.at[c, left, :, pl.ds(0, half)], right),
            across(9, c, hid.at[c, right, :, pl.ds(half, half)], hid.at[c, right, :, pl.ds(half, half)], left),
        )

    def onward_in(c):
        return (
            across(8, c, hid.at[c, opp, :, pl.ds(0, half)], hid.at[c, opp, :, pl.ds(0, half)], right),
            across(9, c, hid.at[c, opp, :, pl.ds(half, half)], hid.at[c, opp, :, pl.ds(half, half)], left),
        )

    def start(copies):
        for copy in copies:
            copy.start()

    def arrive(copies):
        for copy in copies:
            copy.wait_recv()

    def multiply(c):
        group = recv.at[pl.ds(c * SPAN, SPAN)]
        pltpu.make_async_copy(group, group, recv_sem.at[c]).wait()
        tiles = unpack(recv, c)
        x = jnp.concatenate(
            [
                jnp.concatenate(
                    [tiles[64 * b : 64 * b + 64, LANES * q : LANES * (q + 1)] for b in range(BLOCKS)],
                    axis=1,
                )
                for q in range(QUADS)
            ],
            axis=0,
        )
        for side, w in enumerate((wg, wu)):
            product = dot_t(x, w[...])
            for owner in range(n_rep):
                share = product[quarter * owner : quarter * (owner + 1)]
                part[side, c, owner] = share
                part16[side, c, owner] = share.astype(BF16)
        start(far(c))
        start(near(c))

    def add_on(c):
        arrive(far(c))
        relay[0, c] = (part[0, c, right] + far_in[0, c].astype(F32)).astype(BF16)
        relay[1, c] = (part[1, c, left] + far_in[1, c].astype(F32)).astype(BF16)
        start(relayed(c))

    def activate(c):
        arrive(near(c))
        arrive(relayed(c))
        gate = part[0, c, rep] + near_in[0, c].astype(F32) + relay_in[0, c].astype(F32)
        up = part[1, c, rep] + near_in[1, c].astype(F32) + relay_in[1, c].astype(F32)
        hid[c, rep] = (gate / (1.0 + jnp.exp(-gate)) * up).astype(BF16)
        start(hidden_out(c))

    def forward(c):
        arrive(hidden_in(c))
        start(onward(c))

    def down(c):
        arrive(onward_in(c))
        rows2d = dot(hid[c].reshape(n_rep * quarter, ff), wd[...]).astype(BF16)
        pack(rows2d, back, c)

        @pl.loop(0, SPAN)
        def _(h):
            k = c * SPAN + h

            @pl.when(k > 0)
            def _():
                pltpu.make_async_remote_copy(
                    src_ref=back.at[k],
                    dst_ref=home.at[k],
                    send_sem=back_sem,
                    recv_sem=home_sem.at[c],
                    device_id={"exp": peer(k, -1)},
                    device_id_type=MESH,
                ).start()

            @pl.when(k == 0)
            def _():
                pltpu.make_async_copy(back.at[0], home.at[0], home_sem.at[0]).start()

    @pl.loop(0, n_z + STAGES - 1)
    def _(i):
        for age, stage in ((4, down), (3, forward), (2, activate), (1, add_on), (0, multiply)):

            @pl.when((i >= age) & (i < n_z + age))
            def _(age=age, stage=stage):
                stage(i - age)

    @pl.loop(0, n_z)
    def _(c):
        group = home.at[pl.ds(c * SPAN, SPAN)]
        pltpu.make_async_copy(group, group, home_sem.at[c]).wait()
        tiles = unpack(home, c)
        for q in range(QUADS):
            for s in range(4):
                for b in range(BLOCKS):
                    table[
                        pl.ds((4 * q + s) * experts + c * SPAN, SPAN), LANES * b : LANES * (b + 1)
                    ] = tiles[64 * b + 16 * s : 64 * b + 16 * s + 16, LANES * q : LANES * (q + 1)]

    slot, prob = slot_tok[...], prob_tok[...]
    mix = jnp.concatenate(
        [jnp.where(slot == float(s), prob, 0.0) for s in range(CAP)], axis=1
    )
    high = mix.astype(BF16)
    low = (mix - high.astype(F32)).astype(BF16)
    out[...] = (dot(high, table[...]) + dot(low, table[...])).astype(BF16)

    sent = send.at[pl.ds(1, experts - 1)]
    pltpu.make_async_copy(sent, sent, send_sem).wait()
    returned = back.at[pl.ds(1, experts - 1)]
    pltpu.make_async_copy(returned, returned, back_sem).wait()

    @pl.loop(0, n_z)
    def _(c):
        for copies in (far(c), near(c), relayed(c), hidden_out(c), onward(c)):
            for copy in copies:
                copy.wait_send()


def local(sizes, tokens, expert_ids, route_weights, w_gate, w_up, w_down):
    n_z, n_y, n_rep = sizes
    experts = n_z * SPAN
    rows, width = tokens.shape
    ff = w_gate.shape[1]
    quarter = SPAN * CAP // n_rep
    messages = pltpu.VMEM((experts, QUADS, SPAN, LANES), BF16)
    pair = pltpu.VMEM((2, n_z, quarter, ff), BF16)
    vmem = pl.BlockSpec(memory_space=pltpu.VMEM)
    anywhere = pl.BlockSpec(memory_space=pl.ANY)
    return pl.pallas_call(
        functools.partial(kernel, sizes),
        out_shape=jax.ShapeDtypeStruct((rows, width), BF16),
        in_specs=[vmem] * 3 + [anywhere] * 3,
        out_specs=vmem,
        scratch_shapes=[
            pltpu.VMEM((ff, width), BF16),
            pltpu.VMEM((ff, width), BF16),
            pltpu.VMEM((ff, width), BF16),
            pltpu.VMEM((256, 256), BF16),
            pltpu.VMEM((256, 256), BF16),
            pltpu.VMEM((experts, rows), F32),
            pltpu.VMEM((rows, experts), F32),
            pltpu.VMEM((rows, experts), F32),
            messages,
            messages,
            messages,
            messages,
            pltpu.VMEM((CAP * experts, width), BF16),
            pltpu.VMEM((2, n_z, n_rep, quarter, ff), F32),
            pltpu.VMEM((2, n_z, n_rep, quarter, ff), BF16),
            pair,
            pair,
            pair,
            pair,
            pltpu.VMEM((n_z, n_rep, quarter, ff), BF16),
            pltpu.SemaphoreType.DMA((3,)),
            pltpu.SemaphoreType.DMA,
            pltpu.SemaphoreType.DMA((n_z,)),
            pltpu.SemaphoreType.DMA,
            pltpu.SemaphoreType.DMA((n_z,)),
            pltpu.SemaphoreType.DMA((10, n_z)),
            pltpu.SemaphoreType.DMA((10, n_z)),
        ],
        compiler_params=pltpu.CompilerParams(
            collective_id=0, has_side_effects=True, vmem_limit_bytes=58 * 1024 * 1024
        ),
    )(tokens, expert_ids, route_weights, w_gate, w_up, w_down)


def solution(mesh):
    n_rep, experts = mesh.shape["rep"], mesh.shape["exp"]
    sizes = (experts // SPAN, SPAN // CORES, n_rep)
    return jax.shard_map(
        functools.partial(local, sizes),
        mesh=mesh,
        in_specs=(
            P("exp", "rep"),
            P("exp", None),
            P("exp", None),
            P("exp", None, "rep"),
            P("exp", None, "rep"),
            P("exp", None, "rep"),
        ),
        out_specs=P("exp", "rep"),
        check_vma=False,
    )
```

time: 257 us -> 134 us (0.52)
  Pallas kernels: 0 us -> 130 us
  blocking collectives: 105 us -> 0 us
  waiting for transfers between devices: 84 us -> 0 us
  local copies, waits for them, and re-layouts: 24.9 us -> 3.73 us
  starting transfers between devices: 15.8 us -> 0 us
  between operations: 13.3 us -> 0.01 us
  matrix products: 10.7 us -> 0 us
    pallas_call x0 -> x1, Pallas kernels: none -> 130 us  [local(): pl.pallas_call(functools.partial(kernel, sizes), out_shape=jax.ShapeDtype...]
    all_to_all x2 -> x0, blocking collectives: 94 us -> none  [the longest x1 71.6 us: local(): lax.all_to_all(outgoing, 'exp', split_axis=0, concat_axis=1, tiled=True)]
    all_to_all x1 -> x0, waiting for transfers between devices: 41.1 us -> none  [local(): lax.all_to_all(lax.all_to_all(split_out, 'rep', split_axis=3, concat_axis...]
    all_gather x3 -> x0, waiting for transfers between devices: 40.8 us -> none  [the longest x1 40.8 us: local(): lax.all_gather(w_down, 'rep', axis=2, tiled=True)]
    all_to_all x1 -> x0, starting transfers between devices: 15.7 us -> none  [local(): lax.all_to_all(lax.all_to_all(split_out, 'rep', split_axis=3, concat_axis...]
    all_gather x1 -> x0, blocking collectives: 11.1 us -> none  [local(): full_rows = lax.all_gather(tokens, 'rep', axis=1, tiled=True)]
    dot_general x2 -> x0, matrix products: 10.7 us -> none  [the longest x1 6.33 us: local(): jnp.einsum('esf,efd->esd', hidden, lax.all_gather(w_down, 'rep', axis=2,...]
    scatter x1 -> x0, local copies, waits for them, and re-layouts: 7.66 us -> none  [local(): outgoing = jnp.zeros((EXPERTS * slot_cap, width), jnp.bfloat16).at[destin...]
  transfers between devices with their start and end apart: 4 -> 0, of which waited for: 2 -> 0; matrix products, arithmetic and copies ran while one was open for 8% -> 0% of each run, Pallas kernels for 0% -> 0%
where the time goes in v1:
time: 134 us; the launch traced here: 133 us
  Pallas kernels  130 us (97%)
  local copies, waits for them, and re-layouts  3.73 us (3%)
    pallas_call x1, Pallas kernels, local(): pl.pallas_call(functools.partial(kernel, sizes), out_shape=jax.ShapeDtype...  130 us
    unnamed x5, local copies, waits for them, and re-layouts  3.73 us

profile of v1, /device:TPU:1, one launch (start us, length us, event | category | flops | bytes accessed | tf_op | source)
XLA Modules:
  0.0 133.4 jit_solution(5583967720585132799)
XLA Ops:
  0.0 0.0 copy-start
  0.0 1.4 %copy.7.ids = s32[128,8]{1,0:T(8,128)} copy(s32[128,8]{0,1:T(8,128)} %param.7) | data formatting | bytes 8192 | tf_op args[1]
  1.4 0.0 copy-done
  1.4 0.7 copy.8.route
  2.2 129.7 %shard_map.64 = bf16[128,512]{1,0:T(8,128)(2,1)} custom-call(bf16[128,512]{1,0:T(8,128)(2,1)} %tok.1, s32[128,8]{1,0:T(8,128)} %copy.7.ids, f32[128,8]{1,0:T(8,128)} %copy.8.route, bf16[1,768,512]{2,1,0:T(8,128)(2,1)} %wg_any.1, bf16[1,768,512]{2,1,0:T(8,128)(2,1)} %wu_any.1, bf16[1,768,512]{2,1,0:T(8,128)(2,1)} %wd_any.1), custom_call_target="tpu_custom_call" | custom-call | tf_op jit(solution)/shard_map/pallas_call | solution.py:370
  131.8 1.6 %copy.10 = bf16[128,512]{1,0:T(8,128)(2,1)} copy(bf16[128,512]{1,0:T(8,128)(2,1)} %shard_map.64) | data formatting | bytes 262144
Async XLA Ops:
  0.0 1.4 %copy-start = (f32[128,8]{0,1:T(8,128)S(1)}, f32[128,8]{0,1:T(8,128)}, u32[]{:S(2)}) copy-start(f32[128,8]{0,1:T(8,128)} %param.8) | copy-start | bytes 12292

commit v2 on v1

--- a/solution.py
+++ b/solution.py
@@ -19,8 +19,11 @@
 STAGES = 5
 
 
-def signed_step(place, size):
-    return (size + (1 - 2 * ((place + 1) % 2)) * ((place + 1) // 2)) % size
+def signed_step(place):
+    after = place + 1
+    if isinstance(place, int):
+        return (1 - 2 * (after % 2)) * (after // 2)
+    return (1 - 2 * lax.rem(after, 2)) * lax.div(after, 2)
 
 
 def place_of(offset, size):
@@ -52,8 +55,7 @@
     perm,
     perm_t,
     slot_t,
-    slot_tok,
-    prob_tok,
+    prob_t,
     send,
     recv,
     back,
@@ -80,20 +82,37 @@
     half = ff // 2
     quarter = SPAN * CAP // n_rep
     me, rep = lax.axis_index("exp"), lax.axis_index("rep")
-    my_z, my_y, my_c = me // SPAN, (me // CORES) % n_y, me % CORES
-    right, left, opp = (rep + 1) % n_rep, (rep + n_rep - 1) % n_rep, (rep + 2) % n_rep
-
-    def peer(k, sign):
-        place_z, place_y, flip = k // SPAN, (k % SPAN) // CORES, k % CORES
-        z = (my_z + n_z + sign * signed_step(place_z, n_z)) % n_z
-        y = (my_y + n_y + sign * signed_step(place_y, n_y)) % n_y
-        return (z * n_y + y) * CORES + (my_c + flip) % CORES
+    my_z, my_y, my_c = lax.div(me, SPAN), lax.rem(lax.div(me, CORES), n_y), lax.rem(me, CORES)
+    right, left, opp = (lax.rem(rep + step, n_rep) for step in (1, n_rep - 1, 2))
+
+    def spots(sign):
+        return [
+            lax.rem(my_y + n_y + sign * signed_step(h // CORES), n_y) * CORES
+            + lax.rem(my_c + h % CORES, CORES)
+            for h in range(SPAN)
+        ]
+
+    def plane(g, sign):
+        return lax.rem(my_z + n_z + sign * signed_step(g), n_z) * SPAN
+
+    ahead, behind = spots(1), spots(-1)
 
     barrier = pltpu.get_barrier_semaphore()
 
-    @pl.loop(1, experts)
-    def _(k):
-        pl.semaphore_signal(barrier, inc=1, device_id={"exp": peer(k, 1)}, device_id_type=MESH)
+    @pl.loop(0, n_z)
+    def _(g):
+        base = plane(g, 1)
+        for h in range(SPAN):
+
+            def greet(h=h):
+                pl.semaphore_signal(
+                    barrier, inc=1, device_id={"exp": base + ahead[h]}, device_id_type=MESH
+                )
+
+            if h:
+                greet()
+            else:
+                pl.when(g > 0)(greet)
 
     for side in (left, right):
         pl.semaphore_signal(barrier, inc=1, device_id={"rep": side}, device_id_type=MESH)
@@ -115,29 +134,49 @@
     ).astype(F32).astype(BF16)
 
     chosen = ids[...]
-    rows = chosen.shape[0]
+    rows = chosen.shape[1]
     off_z = ((chosen >> 4) - my_z + n_z) & (n_z - 1)
     off_y = (((chosen >> 1) & (n_y - 1)) - my_y + n_y) & (n_y - 1)
     off_c = ((chosen & 1) - my_c + CORES) & 1
     number = place_of(off_z, n_z) * SPAN + place_of(off_y, n_y) * CORES + off_c
-    probs = route[...] / jnp.sum(route[...], axis=1, keepdims=True)
-    lane = lax.broadcasted_iota(jnp.int32, (rows, experts), 1)
-    named = jnp.zeros((rows, experts), F32)
-    prob = jnp.zeros((rows, experts), F32)
-    for j in range(chosen.shape[1]):
-        hit = number[:, j : j + 1] == lane
+    probs = route[...] / jnp.sum(route[...], axis=0, keepdims=True)
+    place = lax.broadcasted_iota(jnp.int32, (experts, rows), 0)
+    named = jnp.zeros((experts, rows), F32)
+    prob = jnp.zeros((experts, rows), F32)
+    for j in range(chosen.shape[0]):
+        hit = number[j : j + 1, :] == place
         named = named + jnp.where(hit, 1.0, 0.0)
-        prob = prob + jnp.where(hit, probs[:, j : j + 1], 0.0)
+        prob = prob + jnp.where(hit, probs[j : j + 1, :], 0.0)
     t_row = lax.broadcasted_iota(jnp.int32, (rows, rows), 0)
     t_col = lax.broadcasted_iota(jnp.int32, (rows, rows), 1)
-    below = (t_col < t_row).astype(F32).astype(BF16)
-    slot = dot(below, named.astype(BF16))
-    slot = jnp.where(named > 0.5, slot, -1.0)
-    slot_tok[...] = slot
-    prob_tok[...] = prob
-    slot_t[...] = slot.T
+    earlier = (t_row < t_col).astype(F32).astype(BF16)
+    slot_t[...] = jnp.where(named > 0.5, dot(named.astype(BF16), earlier), -1.0)
+    prob_t[...] = prob
 
     pl.semaphore_wait(barrier, experts + 1)
+
+    def deliver(g, sign, spot, src, dst, out_sem, in_sem):
+        base = plane(g, sign)
+        for h in range(SPAN):
+
+            def go(h=h):
+                pltpu.make_async_remote_copy(
+                    src_ref=src.at[g * SPAN + h],
+                    dst_ref=dst.at[g * SPAN + h],
+                    send_sem=out_sem,
+                    recv_sem=in_sem.at[g],
+                    device_id={"exp": base + spot[h]},
+                    device_id_type=MESH,
+                ).start()
+
+            if h:
+                go()
+            else:
+                pl.when(g > 0)(go)
+
+                @pl.when(g == 0)
+                def _():
+                    pltpu.make_async_copy(src.at[0], dst.at[0], in_sem.at[0]).start()
 
     def pack(rows2d, place, g):
         stacked = jnp.concatenate(
@@ -170,24 +209,7 @@
         )
         pack(dot(onehot, tok[...]).astype(BF16), send, g)
 
-        @pl.loop(0, SPAN)
-        def _(h):
-            k = g * SPAN + h
-
-            @pl.when(k > 0)
-            def _():
-                pltpu.make_async_remote_copy(
-                    src_ref=send.at[k],
-                    dst_ref=recv.at[k],
-                    send_sem=send_sem,
-                    recv_sem=recv_sem.at[g],
-                    device_id={"exp": peer(k, 1)},
-                    device_id_type=MESH,
-                ).start()
-
-            @pl.when(k == 0)
-            def _():
-                pltpu.make_async_copy(send.at[0], recv.at[0], recv_sem.at[0]).start()
+        deliver(g, 1, ahead, send, recv, send_sem, recv_sem)
 
     for copy in weights:
         copy.wait()
@@ -298,24 +320,7 @@
         rows2d = dot(hid[c].reshape(n_rep * quarter, ff), wd[...]).astype(BF16)
         pack(rows2d, back, c)
 
-        @pl.loop(0, SPAN)
-        def _(h):
-            k = c * SPAN + h
-
-            @pl.when(k > 0)
-            def _():
-                pltpu.make_async_remote_copy(
-                    src_ref=back.at[k],
-                    dst_ref=home.at[k],
-                    send_sem=back_sem,
-                    recv_sem=home_sem.at[c],
-                    device_id={"exp": peer(k, -1)},
-                    device_id_type=MESH,
-                ).start()
-
-            @pl.when(k == 0)
-            def _():
-                pltpu.make_async_copy(back.at[0], home.at[0], home_sem.at[0]).start()
+        deliver(c, -1, behind, back, home, back_sem, home_sem)
 
     @pl.loop(0, n_z + STAGES - 1)
     def _(i):
@@ -337,7 +342,7 @@
                         pl.ds((4 * q + s) * experts + c * SPAN, SPAN), LANES * b : LANES * (b + 1)
                     ] = tiles[64 * b + 16 * s : 64 * b + 16 * s + 16, LANES * q : LANES * (q + 1)]
 
-    slot, prob = slot_tok[...], prob_tok[...]
+    slot, prob = slot_t[...].T, prob_t[...].T
     mix = jnp.concatenate(
         [jnp.where(slot == float(s), prob, 0.0) for s in range(CAP)], axis=1
     )
@@ -379,8 +384,7 @@
             pltpu.VMEM((256, 256), BF16),
             pltpu.VMEM((256, 256), BF16),
             pltpu.VMEM((experts, rows), F32),
-            pltpu.VMEM((rows, experts), F32),
-            pltpu.VMEM((rows, experts), F32),
+            pltpu.VMEM((experts, rows), F32),
             messages,
             messages,
             messages,
@@ -404,7 +408,7 @@
         compiler_params=pltpu.CompilerParams(
             collective_id=0, has_side_effects=True, vmem_limit_bytes=58 * 1024 * 1024
         ),
-    )(tokens, expert_ids, route_weights, w_gate, w_up, w_down)
+    )(tokens, expert_ids.T, route_weights.T, w_gate, w_up, w_down)
 
 
 def solution(mesh):

time: 134 us -> 128 us (0.955); the launches traced: 133 us -> 126 us
  Pallas kernels: 130 us -> 124 us
  local copies, waits for them, and re-layouts: 3.73 us -> 1.57 us
    pallas_call x1, Pallas kernels: 130 us -> 124 us  [local(): pl.pallas_call(functools.partial(kernel, sizes), out_shape=jax.ShapeDtype...]
    unnamed x5 -> x1, local copies, waits for them, and re-layouts: 3.73 us -> 1.57 us
where the time goes in v2:
time: 128 us; the launch traced here: 126 us
  Pallas kernels  124 us (97%)
  local copies, waits for them, and re-layouts  1.57 us (1%)
    pallas_call x1, Pallas kernels, local(): pl.pallas_call(functools.partial(kernel, sizes), out_shape=jax.ShapeDtype...  124 us

profile of v2, /device:TPU:1, one launch (start us, length us, event | category | flops | bytes accessed | tf_op | source)
XLA Modules:
  0.0 126.0 jit_solution(14635145582927494941)
XLA Ops:
  0.0 124.5 %shard_map.64 = bf16[128,512]{1,0:T(8,128)(2,1)} custom-call(bf16[128,512]{1,0:T(8,128)(2,1)} %tok.1, s32[8,128]{1,0:T(8,128)} %bitcast.2, f32[8,128]{1,0:T(8,128)} %bitcast.3, bf16[1,768,512]{2,1,0:T(8,128)(2,1)} %wg_any.1, bf16[1,768,512]{2,1,0:T(8,128)(2,1)} %wu_any.1, bf16[1,768,512]{2,1,0:T(8,128)(2,1)} %wd_any.1), custom_call_target="tpu_custom_call" | custom-call | tf_op jit(solution)/shard_map/pallas_call | solution.py:375
  124.5 1.6 %copy.8 = bf16[128,512]{1,0:T(8,128)(2,1)} copy(bf16[128,512]{1,0:T(8,128)(2,1)} %shard_map.64) | data formatting | bytes 262144

commit v3 on v2

--- a/solution.py
+++ b/solution.py
@@ -17,19 +17,6 @@
 BLOCKS = 4
 CORES = 2
 STAGES = 5
-
-
-def signed_step(place):
-    after = place + 1
-    if isinstance(place, int):
-        return (1 - 2 * (after % 2)) * (after // 2)
-    return (1 - 2 * lax.rem(after, 2)) * lax.div(after, 2)
-
-
-def place_of(offset, size):
-    return jnp.where(
-        offset == 0, 0, jnp.where(2 * offset <= size, 2 * offset - 1, 2 * (size - offset))
-    )
 
 
 def dot(a, b):
@@ -87,32 +74,33 @@
 
     def spots(sign):
         return [
-            lax.rem(my_y + n_y + sign * signed_step(h // CORES), n_y) * CORES
+            lax.rem(my_y + n_y + sign * (h // CORES), n_y) * CORES
             + lax.rem(my_c + h % CORES, CORES)
             for h in range(SPAN)
         ]
 
-    def plane(g, sign):
-        return lax.rem(my_z + n_z + sign * signed_step(g), n_z) * SPAN
-
     ahead, behind = spots(1), spots(-1)
+    order = sorted(range(SPAN), key=lambda h: min(h // CORES, n_y - h // CORES))
+
+    def each(g, sign, spot, act):
+        planes = [
+            lax.rem(my_z + n_y * n_z + sign * (g + i), n_z) * SPAN for i in range(SPAN // CORES)
+        ]
+        for h in order:
+            device = planes[h // CORES] + spot[h]
+            if h:
+                act(g * SPAN + h, device)
+            else:
+                pl.when(g > 0)(functools.partial(act, g * SPAN, device))
 
     barrier = pltpu.get_barrier_semaphore()
+
+    def greet(k, device):
+        pl.semaphore_signal(barrier, inc=1, device_id={"exp": device}, device_id_type=MESH)
 
     @pl.loop(0, n_z)
     def _(g):
-        base = plane(g, 1)
-        for h in range(SPAN):
-
-            def greet(h=h):
-                pl.semaphore_signal(
-                    barrier, inc=1, device_id={"exp": base + ahead[h]}, device_id_type=MESH
-                )
-
-            if h:
-                greet()
-            else:
-                pl.when(g > 0)(greet)
+        each(g, 1, ahead, greet)
 
     for side in (left, right):
         pl.semaphore_signal(barrier, inc=1, device_id={"rep": side}, device_id_type=MESH)
@@ -138,7 +126,7 @@
     off_z = ((chosen >> 4) - my_z + n_z) & (n_z - 1)
     off_y = (((chosen >> 1) & (n_y - 1)) - my_y + n_y) & (n_y - 1)
     off_c = ((chosen & 1) - my_c + CORES) & 1
-    number = place_of(off_z, n_z) * SPAN + place_of(off_y, n_y) * CORES + off_c
+    number = ((off_z - off_y) & (n_z - 1)) * SPAN + off_y * CORES + off_c
     probs = route[...] / jnp.sum(route[...], axis=0, keepdims=True)
     place = lax.broadcasted_iota(jnp.int32, (experts, rows), 0)
     named = jnp.zeros((experts, rows), F32)
@@ -156,27 +144,21 @@
     pl.semaphore_wait(barrier, experts + 1)
 
     def deliver(g, sign, spot, src, dst, out_sem, in_sem):
-        base = plane(g, sign)
-        for h in range(SPAN):
-
-            def go(h=h):
-                pltpu.make_async_remote_copy(
-                    src_ref=src.at[g * SPAN + h],
-                    dst_ref=dst.at[g * SPAN + h],
-                    send_sem=out_sem,
-                    recv_sem=in_sem.at[g],
-                    device_id={"exp": base + spot[h]},
-                    device_id_type=MESH,
-                ).start()
-
-            if h:
-                go()
-            else:
-                pl.when(g > 0)(go)
-
-                @pl.when(g == 0)
-                def _():
-                    pltpu.make_async_copy(src.at[0], dst.at[0], in_sem.at[0]).start()
+        @pl.when(g == 0)
+        def _():
+            pltpu.make_async_copy(src.at[0], dst.at[0], in_sem.at[0]).start()
+
+        def go(k, device):
+            pltpu.make_async_remote_copy(
+                src_ref=src.at[k],
+                dst_ref=dst.at[k],
+                send_sem=out_sem,
+                recv_sem=in_sem.at[g],
+                device_id={"exp": device},
+                device_id_type=MESH,
+            ).start()
+
+        each(g, sign, spot, go)
 
     def pack(rows2d, place, g):
         stacked = jnp.concatenate(

time: 128 us -> 118 us (0.922)
  the two profiles are of different devices: /device:TPU:1 before, /device:TPU:25 now
where the time goes in v3:
time: 118 us
  Pallas kernels  116 us (98%)
  local copies, waits for them, and re-layouts  1.57 us (1%)
    pallas_call x1, Pallas kernels, local(): pl.pallas_call(functools.partial(kernel, sizes), out_shape=jax.ShapeDtype...  116 us

profile of v3, /device:TPU:25, one launch (start us, length us, event | category | flops | bytes accessed | tf_op | source)
XLA Modules:
  0.0 117.9 jit_solution(11414648917011467721)
XLA Ops:
  0.0 116.3 %shard_map.64 = bf16[128,512]{1,0:T(8,128)(2,1)} custom-call(bf16[128,512]{1,0:T(8,128)(2,1)} %tok.1, s32[8,128]{1,0:T(8,128)} %bitcast.2, f32[8,128]{1,0:T(8,128)} %bitcast.3, bf16[1,768,512]{2,1,0:T(8,128)(2,1)} %wg_any.1, bf16[1,768,512]{2,1,0:T(8,128)(2,1)} %wu_any.1, bf16[1,768,512]{2,1,0:T(8,128)(2,1)} %wd_any.1), custom_call_target="tpu_custom_call" | custom-call | tf_op jit(solution)/shard_map/pallas_call | solution.py:357
  116.3 1.6 %copy.8 = bf16[128,512]{1,0:T(8,128)(2,1)} copy(bf16[128,512]{1,0:T(8,128)(2,1)} %shard_map.64) | data formatting | bytes 262144

commit v4 on v3

--- a/solution.py
+++ b/solution.py
@@ -17,6 +17,7 @@
 BLOCKS = 4
 CORES = 2
 STAGES = 5
+PLANES = {8: (0, 1, 2, 6, 4, 3, 5, 7), 2: (0, 1), 1: (0,)}
 
 
 def dot(a, b):
@@ -82,25 +83,19 @@
     ahead, behind = spots(1), spots(-1)
     order = sorted(range(SPAN), key=lambda h: min(h // CORES, n_y - h // CORES))
 
-    def each(g, sign, spot, act):
-        planes = [
-            lax.rem(my_z + n_y * n_z + sign * (g + i), n_z) * SPAN for i in range(SPAN // CORES)
-        ]
+    def each(v, sign, spot, act):
+        base = lax.rem(my_z + n_z + sign * PLANES[n_z][v], n_z) * SPAN
         for h in order:
-            device = planes[h // CORES] + spot[h]
-            if h:
-                act(g * SPAN + h, device)
-            else:
-                pl.when(g > 0)(functools.partial(act, g * SPAN, device))
+            if v or h:
+                act(v * SPAN + h, base + spot[h])
 
     barrier = pltpu.get_barrier_semaphore()
 
     def greet(k, device):
         pl.semaphore_signal(barrier, inc=1, device_id={"exp": device}, device_id_type=MESH)
 
-    @pl.loop(0, n_z)
-    def _(g):
-        each(g, 1, ahead, greet)
+    for v in range(n_z):
+        each(v, 1, ahead, greet)
 
     for side in (left, right):
         pl.semaphore_signal(barrier, inc=1, device_id={"rep": side}, device_id_type=MESH)
@@ -126,7 +121,8 @@
     off_z = ((chosen >> 4) - my_z + n_z) & (n_z - 1)
     off_y = (((chosen >> 1) & (n_y - 1)) - my_y + n_y) & (n_y - 1)
     off_c = ((chosen & 1) - my_c + CORES) & 1
-    number = ((off_z - off_y) & (n_z - 1)) * SPAN + off_y * CORES + off_c
+    turn = sum(jnp.where(off_z == offset, v, 0) for v, offset in enumerate(PLANES[n_z]))
+    number = turn * SPAN + off_y * CORES + off_c
     probs = route[...] / jnp.sum(route[...], axis=0, keepdims=True)
     place = lax.broadcasted_iota(jnp.int32, (experts, rows), 0)
     named = jnp.zeros((experts, rows), F32)
@@ -143,9 +139,8 @@
 
     pl.semaphore_wait(barrier, experts + 1)
 
-    def deliver(g, sign, spot, src, dst, out_sem, in_sem):
-        @pl.when(g == 0)
-        def _():
+    def deliver(v, sign, spot, src, dst, out_sem, in_sem):
+        if v == 0:
             pltpu.make_async_copy(src.at[0], dst.at[0], in_sem.at[0]).start()
 
         def go(k, device):
@@ -153,12 +148,12 @@
                 src_ref=src.at[k],
                 dst_ref=dst.at[k],
                 send_sem=out_sem,
-                recv_sem=in_sem.at[g],
+                recv_sem=in_sem.at[v],
                 device_id={"exp": device},
                 device_id_type=MESH,
             ).start()
 
-        each(g, sign, spot, go)
+        each(v, sign, spot, go)
 
     def pack(rows2d, place, g):
         stacked = jnp.concatenate(
@@ -183,8 +178,7 @@
         )
         return dot(perm_t[...], tiles).astype(BF16)
 
-    @pl.loop(0, n_z)
-    def _(g):
+    for g in range(n_z):
         slots = slot_t[pl.ds(g * SPAN, SPAN), :]
         onehot = jnp.concatenate(
             [(slots == float(s)).astype(F32).astype(BF16) for s in range(CAP)], axis=0
@@ -302,7 +296,11 @@
         rows2d = dot(hid[c].reshape(n_rep * quarter, ff), wd[...]).astype(BF16)
         pack(rows2d, back, c)
 
-        deliver(c, -1, behind, back, home, back_sem, home_sem)
+        for v in range(n_z):
+
+            @pl.when(c == v)
+            def _(v=v):
+                deliver(v, -1, behind, back, home, back_sem, home_sem)
 
     @pl.loop(0, n_z + STAGES - 1)
     def _(i):
@@ -312,6 +310,12 @@
             def _(age=age, stage=stage):
                 stage(i - age)
 
+    slot, prob = slot_t[...].T, prob_t[...].T
+    mix = jnp.concatenate(
+        [jnp.where(slot == float(s), prob, 0.0) for s in range(CAP)], axis=1
+    )
+    high = mix.astype(BF16)
+    low = (mix - high.astype(F32)).astype(BF16)
     @pl.loop(0, n_z)
     def _(c):
         group = home.at[pl.ds(c * SPAN, SPAN)]
@@ -324,12 +328,6 @@
                         pl.ds((4 * q + s) * experts + c * SPAN, SPAN), LANES * b : LANES * (b + 1)
                     ] = tiles[64 * b + 16 * s : 64 * b + 16 * s + 16, LANES * q : LANES * (q + 1)]
 
-    slot, prob = slot_t[...].T, prob_t[...].T
-    mix = jnp.concatenate(
-        [jnp.where(slot == float(s), prob, 0.0) for s in range(CAP)], axis=1
-    )
-    high = mix.astype(BF16)
-    low = (mix - high.astype(F32)).astype(BF16)
     out[...] = (dot(high, table[...]) + dot(low, table[...])).astype(BF16)
 
     sent = send.at[pl.ds(1, experts - 1)]

time: 118 us -> 129 us (1.093)
  the two profiles are of different devices: /device:TPU:25 before, /device:TPU:1 now
where the time goes in v4:
time: 129 us; the launch traced here: 128 us
  Pallas kernels  127 us (98%)
  local copies, waits for them, and re-layouts  1.57 us (1%)
    pallas_call x1, Pallas kernels, local(): pl.pallas_call(functools.partial(kernel, sizes), out_shape=jax.ShapeDtype...  127 us

profile of v4, /device:TPU:1, one launch (start us, length us, event | category | flops | bytes accessed | tf_op | source)
XLA Modules:
  0.0 128.3 jit_solution(11885457722542026253)
XLA Ops:
  0.0 126.7 %shard_map.64 = bf16[128,512]{1,0:T(8,128)(2,1)} custom-call(bf16[128,512]{1,0:T(8,128)(2,1)} %tok.1, s32[8,128]{1,0:T(8,128)} %bitcast.2, f32[8,128]{1,0:T(8,128)} %bitcast.3, bf16[1,768,512]{2,1,0:T(8,128)(2,1)} %wg_any.1, bf16[1,768,512]{2,1,0:T(8,128)(2,1)} %wu_any.1, bf16[1,768,512]{2,1,0:T(8,128)(2,1)} %wd_any.1), custom_call_target="tpu_custom_call" | custom-call | tf_op jit(solution)/shard_map/pallas_call | solution.py:355
  126.7 1.6 %copy.8 = bf16[128,512]{1,0:T(8,128)(2,1)} copy(bf16[128,512]{1,0:T(8,128)(2,1)} %shard_map.64) | data formatting | bytes 262144

commit v5 on v4

--- a/solution.py
+++ b/solution.py
@@ -17,7 +17,6 @@
 BLOCKS = 4
 CORES = 2
 STAGES = 5
-PLANES = {8: (0, 1, 2, 6, 4, 3, 5, 7), 2: (0, 1), 1: (0,)}
 
 
 def dot(a, b):
@@ -81,13 +80,15 @@
         ]
 
     ahead, behind = spots(1), spots(-1)
-    order = sorted(range(SPAN), key=lambda h: min(h // CORES, n_y - h // CORES))
+    planes = {
+        sign: [lax.rem(my_z + n_z + sign * offset, n_z) * SPAN for offset in range(n_z)]
+        for sign in (1, -1)
+    }
 
     def each(v, sign, spot, act):
-        base = lax.rem(my_z + n_z + sign * PLANES[n_z][v], n_z) * SPAN
-        for h in order:
+        for h in sorted(range(SPAN), key=lambda h: ((h // 2) * 3 + (h % 2) * 4) % 8 * 2 + h % 2):
             if v or h:
-                act(v * SPAN + h, base + spot[h])
+                act(v * SPAN + h, planes[sign][(h // CORES + v) % n_z] + spot[h])
 
     barrier = pltpu.get_barrier_semaphore()
 
@@ -121,8 +122,7 @@
     off_z = ((chosen >> 4) - my_z + n_z) & (n_z - 1)
     off_y = (((chosen >> 1) & (n_y - 1)) - my_y + n_y) & (n_y - 1)
     off_c = ((chosen & 1) - my_c + CORES) & 1
-    turn = sum(jnp.where(off_z == offset, v, 0) for v, offset in enumerate(PLANES[n_z]))
-    number = turn * SPAN + off_y * CORES + off_c
+    number = ((off_z - off_y) & (n_z - 1)) * SPAN + off_y * CORES + off_c
     probs = route[...] / jnp.sum(route[...], axis=0, keepdims=True)
     place = lax.broadcasted_iota(jnp.int32, (experts, rows), 0)
     named = jnp.zeros((experts, rows), F32)

time: 129 us -> 110 us (0.85)
  Pallas kernels: 127 us -> 108 us
    pallas_call x1, Pallas kernels: 127 us -> 108 us  [local(): pl.pallas_call(functools.partial(kernel, sizes), out_shape=jax.ShapeDtype...]
where the time goes in v5:
time: 110 us
  Pallas kernels  108 us (98%)
  local copies, waits for them, and re-layouts  1.57 us (1%)
    pallas_call x1, Pallas kernels, local(): pl.pallas_call(functools.partial(kernel, sizes), out_shape=jax.ShapeDtype...  108 us

profile of v5, /device:TPU:1, one launch (start us, length us, event | category | flops | bytes accessed | tf_op | source)
XLA Modules:
  0.0 109.7 jit_solution(8128568173624021387)
XLA Ops:
  0.0 108.1 %shard_map.64 = bf16[128,512]{1,0:T(8,128)(2,1)} custom-call(bf16[128,512]{1,0:T(8,128)(2,1)} %tok.1, s32[8,128]{1,0:T(8,128)} %bitcast.2, f32[8,128]{1,0:T(8,128)} %bitcast.3, bf16[1,768,512]{2,1,0:T(8,128)(2,1)} %wg_any.1, bf16[1,768,512]{2,1,0:T(8,128)(2,1)} %wu_any.1, bf16[1,768,512]{2,1,0:T(8,128)(2,1)} %wd_any.1), custom_call_target="tpu_custom_call" | custom-call | tf_op jit(solution)/shard_map/pallas_call | solution.py:355
  108.1 1.6 %copy.8 = bf16[128,512]{1,0:T(8,128)(2,1)} copy(bf16[128,512]{1,0:T(8,128)(2,1)} %shard_map.64) | data formatting | bytes 262144

commit v6 on v5

--- a/solution.py
+++ b/solution.py
@@ -17,6 +17,32 @@
 BLOCKS = 4
 CORES = 2
 STAGES = 5
+
+
+def chunks_of(n_z, n_y):
+    if n_z != n_y:
+        return [[((i + v) % n_z, i) for i in range(n_y)] for v in range(n_z)]
+
+    def far(offset):
+        return min(offset, n_z - offset)
+
+    left = sorted(
+        ((z, y) for z in range(n_z) for y in range(n_y)),
+        key=lambda p: (far(p[0]) + far(p[1]), abs(far(p[0]) - far(p[1])), p),
+    )
+    chunks = [[] for _ in range(n_z)]
+    chunks[-1], chunks[0] = left[:n_y], left[n_y : 2 * n_y]
+    for z, y in reversed(left[2 * n_y :]):
+
+        def cost(chunk):
+            along_z = sum(far(p[0]) for p in chunk) + far(z)
+            along_y = sum(far(p[1]) for p in chunk) + far(y)
+            same = sum((p[0] == z) + (p[1] == y) for p in chunk)
+            return along_z**2 + along_y**2 + 40 * same
+
+        open_chunks = [chunk for chunk in chunks[1:-1] if len(chunk) < n_y]
+        min(open_chunks, key=cost).append((z, y))
+    return [sorted(chunk, key=lambda p: (p[1], p[0])) for chunk in chunks]
 
 
 def dot(a, b):
@@ -72,23 +98,31 @@
     my_z, my_y, my_c = lax.div(me, SPAN), lax.rem(lax.div(me, CORES), n_y), lax.rem(me, CORES)
     right, left, opp = (lax.rem(rep + step, n_rep) for step in (1, n_rep - 1, 2))
 
-    def spots(sign):
-        return [
-            lax.rem(my_y + n_y + sign * (h // CORES), n_y) * CORES
-            + lax.rem(my_c + h % CORES, CORES)
-            for h in range(SPAN)
-        ]
-
-    ahead, behind = spots(1), spots(-1)
-    planes = {
-        sign: [lax.rem(my_z + n_z + sign * offset, n_z) * SPAN for offset in range(n_z)]
-        for sign in (1, -1)
-    }
-
-    def each(v, sign, spot, act):
+    way = [1 - 2 * my_c, 2 * my_c - 1]
+
+    out_ways, back_ways = [way[0]] * CORES, [-way[0], -way[1]]
+    chunks = chunks_of(n_z, n_y)
+
+    def levels(ways):
+        return (
+            [[lax.rem(my_z + n_z + w * step, n_z) * SPAN for step in range(n_z)] for w in ways],
+            [
+                [
+                    lax.rem(my_y + n_y + w * step, n_y) * CORES + lax.rem(my_c + flip, CORES)
+                    for step in range(n_y)
+                ]
+                for flip, w in enumerate(ways)
+            ],
+        )
+
+    parts = {1: levels(out_ways), -1: levels(back_ways)}
+
+    def each(v, sign, act):
+        in_z, in_y = parts[sign]
         for h in sorted(range(SPAN), key=lambda h: ((h // 2) * 3 + (h % 2) * 4) % 8 * 2 + h % 2):
-            if v or h:
-                act(v * SPAN + h, planes[sign][(h // CORES + v) % n_z] + spot[h])
+            (z, y), flip = chunks[v][h // CORES], h % CORES
+            if z or y or flip:
+                act(v * SPAN + h, in_z[flip][z] + in_y[flip][y])
 
     barrier = pltpu.get_barrier_semaphore()
 
@@ -96,7 +130,7 @@
         pl.semaphore_signal(barrier, inc=1, device_id={"exp": device}, device_id_type=MESH)
 
     for v in range(n_z):
-        each(v, 1, ahead, greet)
+        each(v, 1, greet)
 
     for side in (left, right):
         pl.semaphore_signal(barrier, inc=1, device_id={"rep": side}, device_id_type=MESH)
@@ -119,10 +153,15 @@
 
     chosen = ids[...]
     rows = chosen.shape[1]
-    off_z = ((chosen >> 4) - my_z + n_z) & (n_z - 1)
-    off_y = (((chosen >> 1) & (n_y - 1)) - my_y + n_y) & (n_y - 1)
+    off_z = (way[0] * ((chosen >> 4) - my_z)) & (n_z - 1)
+    off_y = (way[0] * (((chosen >> 1) & (n_y - 1)) - my_y)) & (n_y - 1)
     off_c = ((chosen & 1) - my_c + CORES) & 1
-    number = ((off_z - off_y) & (n_z - 1)) * SPAN + off_y * CORES + off_c
+    number = off_c
+    for v, chunk in enumerate(chunks):
+        for i, (z, y) in enumerate(chunk):
+            number = number + jnp.where(
+                off_z * n_y + off_y == z * n_y + y, v * SPAN + i * CORES, 0
+            )
     probs = route[...] / jnp.sum(route[...], axis=0, keepdims=True)
     place = lax.broadcasted_iota(jnp.int32, (experts, rows), 0)
     named = jnp.zeros((experts, rows), F32)
@@ -139,9 +178,10 @@
 
     pl.semaphore_wait(barrier, experts + 1)
 
-    def deliver(v, sign, spot, src, dst, out_sem, in_sem):
-        if v == 0:
-            pltpu.make_async_copy(src.at[0], dst.at[0], in_sem.at[0]).start()
+    def deliver(v, sign, src, dst, out_sem, in_sem):
+        if (0, 0) in chunks[v]:
+            own = v * SPAN + CORES * chunks[v].index((0, 0))
+            pltpu.make_async_copy(src.at[own], dst.at[own], in_sem.at[v]).start()
 
         def go(k, device):
             pltpu.make_async_remote_copy(
@@ -153,7 +193,7 @@
                 device_id_type=MESH,
             ).start()
 
-        each(v, sign, spot, go)
+        each(v, sign, go)
 
     def pack(rows2d, place, g):
         stacked = jnp.concatenate(
@@ -185,7 +225,7 @@
         )
         pack(dot(onehot, tok[...]).astype(BF16), send, g)
 
-        deliver(g, 1, ahead, send, recv, send_sem, recv_sem)
+        deliver(g, 1, send, recv, send_sem, recv_sem)
 
     for copy in weights:
         copy.wait()
@@ -300,7 +340,7 @@
 
             @pl.when(c == v)
             def _(v=v):
-                deliver(v, -1, behind, back, home, back_sem, home_sem)
+                deliver(v, -1, back, home, back_sem, home_sem)
 
     @pl.loop(0, n_z + STAGES - 1)
     def _(i):

time: 110 us -> 103 us (0.936)
  Pallas kernels: 108 us -> 101 us
    pallas_call x1, Pallas kernels: 108 us -> 101 us  [local(): pl.pallas_call(functools.partial(kernel, sizes), out_shape=jax.ShapeDtype...]
where the time goes in v6:
time: 103 us
  Pallas kernels  101 us (98%)
  local copies, waits for them, and re-layouts  1.57 us (2%)
    pallas_call x1, Pallas kernels, local(): pl.pallas_call(functools.partial(kernel, sizes), out_shape=jax.ShapeDtype...  101 us

profile of v6, /device:TPU:1, one launch (start us, length us, event | category | flops | bytes accessed | tf_op | source)
XLA Modules:
  0.0 102.6 jit_solution(16963531948633468460)
XLA Ops:
  0.0 101.0 %shard_map.64 = bf16[128,512]{1,0:T(8,128)(2,1)} custom-call(bf16[128,512]{1,0:T(8,128)(2,1)} %tok.1, s32[8,128]{1,0:T(8,128)} %bitcast.2, f32[8,128]{1,0:T(8,128)} %bitcast.3, bf16[1,768,512]{2,1,0:T(8,128)(2,1)} %wg_any.1, bf16[1,768,512]{2,1,0:T(8,128)(2,1)} %wu_any.1, bf16[1,768,512]{2,1,0:T(8,128)(2,1)} %wd_any.1), custom_call_target="tpu_custom_call" | custom-call | tf_op jit(solution)/shard_map/pallas_call | solution.py:395
  101.0 1.6 %copy.8 = bf16[128,512]{1,0:T(8,128)(2,1)} copy(bf16[128,512]{1,0:T(8,128)(2,1)} %shard_map.64) | data formatting | bytes 262144

commit v7 on v6

--- a/solution.py
+++ b/solution.py
@@ -129,7 +129,7 @@
     def greet(k, device):
         pl.semaphore_signal(barrier, inc=1, device_id={"exp": device}, device_id_type=MESH)
 
-    for v in range(n_z):
+    for v in (*range(1, n_z), 0):
         each(v, 1, greet)
 
     for side in (left, right):
@@ -368,7 +368,8 @@
                         pl.ds((4 * q + s) * experts + c * SPAN, SPAN), LANES * b : LANES * (b + 1)
                     ] = tiles[64 * b + 16 * s : 64 * b + 16 * s + 16, LANES * q : LANES * (q + 1)]
 
-    out[...] = (dot(high, table[...]) + dot(low, table[...])).astype(BF16)
+    both = dot(jnp.concatenate([high, low], axis=0), table[...])
+    out[...] = (both[: both.shape[0] // 2] + both[both.shape[0] // 2 :]).astype(BF16)
 
     sent = send.at[pl.ds(1, experts - 1)]
     pltpu.make_async_copy(sent, sent, send_sem).wait()

time: 103 us -> 102 us (level)
  no operation moved by 1% of the time
where the time goes in v7:
time: 102 us
  Pallas kernels  101 us (99%)
  local copies, waits for them, and re-layouts  1.57 us (2%)
    pallas_call x1, Pallas kernels, local(): pl.pallas_call(functools.partial(kernel, sizes), out_shape=jax.ShapeDtype...  101 us

profile of v7, /device:TPU:1, one launch (start us, length us, event | category | flops | bytes accessed | tf_op | source)
XLA Modules:
  0.0 102.3 jit_solution(8078183054044973716)
XLA Ops:
  0.0 100.8 %shard_map.64 = bf16[128,512]{1,0:T(8,128)(2,1)} custom-call(bf16[128,512]{1,0:T(8,128)(2,1)} %tok.1, s32[8,128]{1,0:T(8,128)} %bitcast.2, f32[8,128]{1,0:T(8,128)} %bitcast.3, bf16[1,768,512]{2,1,0:T(8,128)(2,1)} %wg_any.1, bf16[1,768,512]{2,1,0:T(8,128)(2,1)} %wu_any.1, bf16[1,768,512]{2,1,0:T(8,128)(2,1)} %wd_any.1), custom_call_target="tpu_custom_call" | custom-call | tf_op jit(solution)/shard_map/pallas_call | solution.py:396
  100.8 1.6 %copy.8 = bf16[128,512]{1,0:T(8,128)(2,1)} copy(bf16[128,512]{1,0:T(8,128)(2,1)} %shard_map.64) | data formatting | bytes 262144
